TPU v7x, 32 devices: a whole 2x2x4 slice. The times are simulated.
32 devices in a mesh: shot: 8 (over z, y), xline: 4 (over x, core).
Axes of the slice: x: 2, y: 2, z: 4, core: 2. Of those that a mesh axis runs over, the one named last changes fastest.
Arguments:
- records: bfloat16 [4, 16, 256, 2048], P('xline', 'shot'), may hold values from -1.796875 to 1.796875
- targets: bfloat16 [2048, 32, 256], P('xline', 'shot'), may hold values from -1.796875 to 1.796875
- aperture: int32 [32, 4, 16], P('shot', 'xline'), may hold values from 0 to 255
Outputs:
- multiples: bfloat16 [2048, 32, 256], P('xline', 'shot')
Inputs may be any that keep to these rules, and one draw needn't show every extreme that they name: An aperture entry is the receiver of the output shot at which the contributing source lies.
All inputs are finite; a program needn't handle non-finite values.
Results may differ from a plain program's by a relative error of at most 0.0071.
Values may be sent and summed in bfloat16 or wider, within the bound.
A program may use at most 128 MiB of HBM per device.

v0:
```python
import math
import jax
import jax.numpy as jnp
from jax import lax
from jax.sharding import PartitionSpec as P

NT = 2048
NF = 256


def forward_table():
    times_col = jnp.arange(NT, dtype=jnp.int32)[:, None]
    freq_row = jnp.arange(1, NF + 1, dtype=jnp.int32)[None, :]
    angles = (times_col * freq_row % NT).astype(jnp.float32) * (2.0 * math.pi / NT)
    normalizing_scale = 1.0 / math.sqrt(NT)
    return jnp.concatenate(
        [jnp.cos(angles) * normalizing_scale, -jnp.sin(angles) * normalizing_scale], axis=1
    ).astype(jnp.bfloat16)


def inverse_table():
    times_col = jnp.arange(NT, dtype=jnp.int32)[:, None]
    freq_row = jnp.arange(1, NF + 1, dtype=jnp.int32)[None, :]
    angles = (times_col * freq_row % NT).astype(jnp.float32) * (2.0 * math.pi / NT)
    normalizing_scale = 2.0 / math.sqrt(NT)
    stacked = jnp.stack(
        [jnp.cos(angles) * normalizing_scale, -jnp.sin(angles) * normalizing_scale], axis=2
    )
    return stacked.reshape(NT, 2 * NF)


def complex_mixing(real_part, imag_part):
    upper = jnp.stack([real_part, -imag_part], axis=1)
    lower = jnp.stack([imag_part, real_part], axis=1)
    return jnp.stack([upper, lower], axis=0)


def on_device(records, targets, aperture):
    forward_fourier = forward_table()
    shots_here = targets.shape[1]
    receivers = targets.shape[2]
    gathered = lax.all_gather(targets, "xline", axis=0, tiled=True)
    desired_spectra = jnp.einsum(
        "tsr,tp->srp", gathered, forward_fourier, preferred_element_type=jnp.float32
    ).astype(jnp.bfloat16)
    held = records.shape[1]
    trace_spectra = jnp.einsum(
        "hwn,ne->hew", records[0], forward_fourier, preferred_element_type=jnp.float32
    )
    trace_spectra = trace_spectra.astype(jnp.bfloat16).reshape(held, 2, NF, receivers)
    selects = aperture[:, 0, :]
    receiver_ids = jnp.arange(receivers, dtype=jnp.int32)
    onehot = (selects[:, :, None] == receiver_ids).astype(jnp.bfloat16)
    picked = jnp.einsum(
        "scr,srp->scp", onehot, desired_spectra, preferred_element_type=jnp.float32
    ).astype(jnp.bfloat16)
    mixing = complex_mixing(picked[:, :, :NF], picked[:, :, NF:])
    running = jnp.einsum(
        "qspcf,cpfr->fqsr",
        mixing,
        lax.all_gather(trace_spectra, "shot", axis=0, tiled=True),
        preferred_element_type=jnp.float32,
    )
    inverse_fourier = inverse_table()
    flat_traces = running.reshape(2 * NF, shots_here * receivers)
    time_rows = NT // lax.axis_size("xline")
    summed = lax.psum(flat_traces, "xline")
    inverse_rows = lax.dynamic_slice_in_dim(
        inverse_fourier, lax.axis_index("xline") * time_rows, time_rows, 0
    )
    local_part = jnp.dot(
        inverse_rows, summed, precision=lax.Precision.HIGHEST, preferred_element_type=jnp.float32
    )
    return local_part.reshape(time_rows, shots_here, receivers).astype(jnp.bfloat16)


def solution(mesh):
    in_specs = (P("xline", "shot", None, None), P("xline", "shot", None), P("shot", "xline", None))
    out_specs = P("xline", "shot", None)
    return jax.shard_map(
        on_device, mesh=mesh, in_specs=in_specs, out_specs=out_specs, check_vma=False
    )
```

profile of v0, /device:TPU:0, one launch (start us, length us, event | category | flops | bytes accessed | tf_op | source)
XLA Modules:
  0.0 191.9 jit_solution(8781376290301886159)
XLA Ops:
  6.5 0.0 copy-start
  6.5 0.0 all-gather.3.cloned.1.call-start
  6.5 0.7 all-gather.3.cloned.1.call-update
  7.3 0.0 all-gather.5.cloned.1.call-start
  7.3 9.1 %multiply_convert_fusion.1 = (bf16[2048,256]{0,1:T(8,128)(2,1)S(1)}, bf16[2048,256]{0,1:T(8,128)(2,1)S(1)}) fusion(s32[256]{0:T(256)S(1)} %iota_add_fusion), kind=kLoop, calls=%fused_computation.21 | loop fusion | flops 9961472 | bytes 2098176 | tf_op jit(solution)/shard_map/convert
  16.4 0.0 copy-start.1
  16.4 0.0 copy-done
  16.4 0.0 copy-start.2
  16.4 2.1 %fusion.24 = bf16[512,2,256]{2,0,1:T(8,128)(2,1)} fusion(bf16[1,2,256,2048]{3,2,1,0:T(8,128)(2,1)S(1)} %copy-done, bf16[2048,256]{0,1:T(8,128)(2,1)S(1)} %get-tuple-element.13, bf16[2048,256]{0,1:T(8,128)(2,1)S(1)} %get-tuple-element.12), kind=kOutput, calls=%fused_computation.33 | convolution fusion | flops 1078198272 | bytes 4718592 | tf_op jit(solution)/shard_map/hwn,ne->hew/dot_general | solution.py:47
  18.6 0.0 copy-done.1
  18.6 0.0 all-gather.5.cloned.1.call-update
  18.6 0.0 all-reduce.2.cloned.1.call-start
  18.6 27.5 %all-gather.3.cloned.1.call-done = bf16[2048,4,256]{2,1,0:T(4,128)(2,1)} async-done(((bf16[512,4,256]{2,1,0:T(4,128)(2,1)}), bf16[2048,4,256]{2,1,0:T(4,128)(2,1)}) %all-gather.3.cloned.1.call-update) | async-done | bytes 4194320 | tf_op jit(solution)/shard_map/all_gather | solution.py:42
  46.2 0.0 copy-done.2
  46.2 5.0 %fusion.30 = bf16[4,16,512]{2,1,0:T(8,128)(2,1)S(1)} fusion(bf16[2048,4,256]{2,1,0:T(4,128)(2,1)} %all-gather.3.cloned.1.call-done, bf16[2048,256]{0,1:T(8,128)(2,1)} %copy-done.1, bf16[2048,256]{0,1:T(8,128)(2,1)S(1)} %get-tuple-element.12, s32[4,16]{1,0:T(4,128)S(1)} %bitcast.49), kind=kOutput, calls=%fused_computation.35 | convolution fusion | flops 2169028608 | bytes 6357248 | tf_op jit(solution)/shard_map/scr,srp->scp/dot_general | solution.py:54
  51.3 1.1 copy.15
  52.4 68.8 %all-gather.5.cloned.1.call-done = bf16[16,2,256,256]{3,2,1,0:T(8,128)(2,1)} async-done(((bf16[2,2,256,256]{3,2,1,0:T(8,128)(2,1)}), bf16[16,2,256,256]{3,2,1,0:T(8,128)(2,1)}) %all-gather.5.cloned.1.call-update) | async-done | bytes 4194320 | tf_op jit(solution)/shard_map/all_gather | solution.py:61
  121.2 5.3 %fusion = f32[256,2,4,256,1]{3,2,4,1,0:T(4,128)S(1)} fusion(bf16[2,4,2,16,256]{3,1,2,0,4:T(4,128)(2,1)S(1)} %copy.15, bf16[16,2,256,256,1]{3,2,1,0,4:T(8,128)(2,1)} %bitcast.47), kind=kOutput, calls=%fused_computation.1 | convolution fusion | flops 33554432 | bytes 6422528 | tf_op jit(solution)/shard_map/qspcf,cpfr->fqsr/dot_general | solution.py:58
  126.5 1.8 copy.22
  128.3 0.0 all-reduce.2.cloned.1.call-update
  128.3 8.5 %cosine_multiply_fusion = (f32[2048,256,1]{1,0,2:T(8,128)S(1)}, f32[2048,256,1]{1,0,2:T(8,128)S(1)}) fusion(s32[256]{0:T(256)S(1)} %iota_add_fusion), kind=kLoop, calls=%fused_computation.25 | loop fusion | flops 8912896 | bytes 4195328 | tf_op jit(solution)/shard_map/mul | solution.py:27
  136.9 2.2 %pad_maximum_fusion = f32[2048,256,2]{1,0,2:T(8,128)} fusion(f32[2048,256,1]{1,0,2:T(8,128)S(1)} %get-tuple-element.11, f32[2048,256,1]{1,0,2:T(8,128)S(1)} %get-tuple-element.10), kind=kLoop, calls=%fused_computation | loop fusion | flops 1048576 | bytes 8388608 | tf_op jit(solution)/shard_map/stack | solution.py:26
  139.1 7.4 %copy.12 = f32[2048,256,2]{0,2,1:T(2,128)} copy(f32[2048,256,2]{1,0,2:T(8,128)} %pad_maximum_fusion) | data formatting | bytes 8388608 | tf_op jit(solution)/shard_map/stack | solution.py:26
  146.5 6.1 %reshape.122 = f32[2048,512]{0,1:T(8,128)} reshape(f32[2048,256,2]{0,2,1:T(2,128)} %copy.12) | data formatting | bytes 8388608 | tf_op jit(solution)/shard_map/reshape | solution.py:29
  152.6 25.8 %all-reduce.2.cloned.1.call-done = f32[512,1024]{1,0:T(8,128)} async-done(((f32[512,1024]{1,0:T(8,128)}), f32[512,1024]{1,0:T(8,128)}) %all-reduce.2.cloned.1.call-update) | async-done | bytes 2097168 | tf_op jit(solution)/shard_map/psum | solution.py:67
  178.4 5.4 %convolution_convert_fusion = bf16[512,1024]{1,0:T(8,128)(2,1)S(1)} fusion(f32[512,1024]{1,0:T(8,128)} %all-reduce.2.cloned.1.call-done, f32[2048,512]{0,1:T(8,128)} %reshape.122, s32[]{:T(128)S(6)} %select_n.30), kind=kOutput, calls=%fused_computation.30 | convolution fusion | flops 3221749760 | bytes 4194308 | tf_op jit(solution)/shard_map/dot_general | solution.py:71
  183.8 1.6 convert_element_type.52
  (4 shorter events, 0.1 us)
Async XLA Ops:
  6.5 9.9 %copy-start = (bf16[1,2,256,2048]{3,2,1,0:T(8,128)(2,1)S(1)}, bf16[1,2,256,2048]{3,2,1,0:T(8,128)(2,1)}, u32[]{:S(2)}) copy-start(bf16[1,2,256,2048]{3,2,1,0:T(8,128)(2,1)} %param.3) | copy-start | bytes 6291460
  6.5 39.6 %all-gather.3.cloned.1.call-start = ((), (), s32[]{:S(2)}) async-start(), calls=%async_computation | async-start | bytes 5242880 | tf_op jit(solution)/shard_map/all_gather | solution.py:42
  7.3 113.9 %all-gather.5.cloned.1.call-start = ((), (), s32[]{:S(2)}) async-start(), calls=%async_computation.1 | async-start | bytes 4718592 | tf_op jit(solution)/shard_map/all_gather | solution.py:61
  16.4 2.2 %copy-start.1 = (bf16[2048,256]{0,1:T(8,128)(2,1)}, bf16[2048,256]{0,1:T(8,128)(2,1)S(1)}, u32[]{:S(2)}) copy-start(bf16[2048,256]{0,1:T(8,128)(2,1)S(1)} %get-tuple-element.13) | copy-start | bytes 3145732
  16.4 29.8 %copy-start.2 = (s32[4,1,16]{2,1,0:T(1,128)S(1)}, s32[4,1,16]{2,1,0:T(1,128)}, u32[]{:S(2)}) copy-start(s32[4,1,16]{2,1,0:T(1,128)} %param.5) | copy-start | bytes 772
  18.6 159.8 %all-reduce.2.cloned.1.call-start = ((), (), s32[]{:S(2)}) async-start(), calls=%async_computation.2 | async-start | bytes 4194304 | tf_op jit(solution)/shard_map/psum | solution.py:67
Sparse Core Ops, SparseCore 0:
  8.9 37.2 all-gather.2
  48.3 72.8 all-gather.4
  128.4 49.9 all-reduce.1
where the time goes:
time: 192 us
  waiting for transfers between devices  123 us (64%)
  other arithmetic  19.9 us (10%)
  local copies, waits for them, and re-layouts  18 us (9%)
  matrix products  17.9 us (9%)
  between operations  13.2 us (7%)
    all_gather x1, waiting for transfers between devices, on_device(): lax.all_gather(trace_spectra, 'shot', axis=0, tiled=True)  68.8 us
    all_gather x1, waiting for transfers between devices, on_device(): gathered = lax.all_gather(targets, 'xline', axis=0, tiled=True)  27.5 us
    psum x1, waiting for transfers between devices, on_device(): summed = lax.psum(flat_traces, 'xline')  25.8 us
    another operation x1, other arithmetic  9.05 us
    mul x1, other arithmetic, inverse_table(): jnp.cos(angles) * normalizing_scale  8.53 us
    another operation x1, local copies, waits for them, and re-layouts, inverse_table(): jnp.stack([jnp.cos(angles) * normalizing_scale, -jnp.sin(angles) * normal...  7.43 us
    reshape x1, local copies, waits for them, and re-layouts, inverse_table(): return stacked.reshape(NT, 2 * NF)  6.09 us
    dot_general x1, matrix products, on_device(): jnp.dot(inverse_rows, summed, precision=lax.Precision.HIGHEST, preferred_...  5.4 us
  transfers between devices with their start and end apart: 3, of which 3 were waited for; matrix products, arithmetic and copies ran while one was open for 22% of the time, Pallas kernels for 0%

commit v1 on v0

--- a/solution.py
+++ b/solution.py
@@ -64,7 +64,8 @@
     inverse_fourier = inverse_table()
     flat_traces = running.reshape(2 * NF, shots_here * receivers)
     time_rows = NT // lax.axis_size("xline")
-    summed = lax.psum(flat_traces, "xline")
+    blocks = lax.all_gather(flat_traces, "xline", axis=0, tiled=False)
+    summed = blocks.sum(axis=0)
     inverse_rows = lax.dynamic_slice_in_dim(
         inverse_fourier, lax.axis_index("xline") * time_rows, time_rows, 0
     )

time: 192 us -> 214 us (1.11)
  waiting for transfers between devices: 123 us -> 130 us
  other arithmetic: 19.9 us -> 26.2 us
  matrix products: 17.9 us -> 22.5 us
  local copies, waits for them, and re-layouts: 18 us -> 22.4 us
    all_gather x0 -> x1, waiting for transfers between devices: none -> 32.3 us  [on_device(): blocks = lax.all_gather(flat_traces, 'xline', axis=0, tiled=False)]
    psum x1 -> x0, waiting for transfers between devices: 25.8 us -> none  [on_device(): summed = lax.psum(flat_traces, 'xline')]
    reduce_sum x0 -> x1, other arithmetic: none -> 5.9 us  [on_device(): summed = blocks.sum(axis=0)]
    another operation x0 -> x1, local copies, waits for them, and re-layouts: none -> 3.32 us  [on_device(): blocks = lax.all_gather(flat_traces, 'xline', axis=0, tiled=False)]
    dot_general x1, matrix products: 5.4 us -> 8.63 us  [on_device(): jnp.dot(inverse_rows, summed, precision=lax.Precision.HIGHEST, preferred_...]
    dot_general x0 -> x1, local copies, waits for them, and re-layouts: none -> 2.91 us  [on_device(): jnp.dot(inverse_rows, summed, precision=lax.Precision.HIGHEST, preferred_...]
  transfers between devices with their start and end apart: 3 -> 3, of which waited for: 3 -> 3; matrix products, arithmetic and copies ran while one was open for 22% -> 20% of each run, Pallas kernels for 0% -> 0%
where the time goes in v1:
time: 214 us
  waiting for transfers between devices  130 us (61%)
  other arithmetic  26.2 us (12%)
  matrix products  22.5 us (11%)
  local copies, waits for them, and re-layouts  22.4 us (10%)
  between operations  13.2 us (6%)
    all_gather x1, waiting for transfers between devices, on_device(): lax.all_gather(trace_spectra, 'shot', axis=0, tiled=True)  68.9 us
    all_gather x1, waiting for transfers between devices, on_device(): blocks = lax.all_gather(flat_traces, 'xline', axis=0, tiled=False)  32.3 us
    all_gather x1, waiting for transfers between devices, on_device(): gathered = lax.all_gather(targets, 'xline', axis=0, tiled=True)  27.5 us
    another operation x1, other arithmetic  9.05 us
    dot_general x1, matrix products, on_device(): jnp.dot(inverse_rows, summed, precision=lax.Precision.HIGHEST, preferred_...  8.63 us
    mul x1, other arithmetic, inverse_table(): jnp.cos(angles) * normalizing_scale  8.31 us
    another operation x1, local copies, waits for them, and re-layouts, inverse_table(): jnp.stack([jnp.cos(angles) * normalizing_scale, -jnp.sin(angles) * normal...  7.42 us
    dot_general x1, matrix products, on_device(): jnp.einsum('qspcf,cpfr->fqsr', mixing, lax.all_gather(trace_spectra, 'sho...  6.68 us
  transfers between devices with their start and end apart: 3, of which 3 were waited for; matrix products, arithmetic and copies ran while one was open for 20% of the time, Pallas kernels for 0%

profile of v1, /device:TPU:0, one launch (start us, length us, event | category | flops | bytes accessed | tf_op | source)
XLA Modules:
  0.0 213.9 jit_solution(6634790961960913567)
XLA Ops:
  6.5 0.0 copy-start
  6.5 0.0 all-gather.4.cloned.1.call-start
  6.5 0.7 all-gather.4.cloned.1.call-update
  7.3 0.0 all-gather.6.cloned.1.call-start
  7.3 9.1 %multiply_convert_fusion.1 = (bf16[2048,256]{0,1:T(8,128)(2,1)S(1)}, bf16[2048,256]{0,1:T(8,128)(2,1)S(1)}) fusion(s32[256]{0:T(256)S(1)} %iota_add_fusion), kind=kLoop, calls=%fused_computation.21 | loop fusion | flops 9961472 | bytes 2098176 | tf_op jit(solution)/shard_map/convert
  16.4 0.0 copy-start.1
  16.4 0.0 copy-done
  16.4 0.0 copy-start.2
  16.4 2.1 %fusion.27 = bf16[512,2,256]{2,0,1:T(8,128)(2,1)} fusion(bf16[1,2,256,2048]{3,2,1,0:T(8,128)(2,1)S(1)} %copy-done, bf16[2048,256]{0,1:T(8,128)(2,1)S(1)} %get-tuple-element.13, bf16[2048,256]{0,1:T(8,128)(2,1)S(1)} %get-tuple-element.12), kind=kOutput, calls=%fused_computation.34 | convolution fusion | flops 1078198272 | bytes 4718592 | tf_op jit(solution)/shard_map/hwn,ne->hew/dot_general | solution.py:47
  18.6 0.0 copy-done.1
  18.6 0.0 all-gather.6.cloned.1.call-update
  18.6 0.0 all-gather.8.cloned.1.call-start
  18.6 27.5 %all-gather.4.cloned.1.call-done = bf16[2048,4,256]{2,1,0:T(4,128)(2,1)} async-done(((bf16[512,4,256]{2,1,0:T(4,128)(2,1)}), bf16[2048,4,256]{2,1,0:T(4,128)(2,1)}) %all-gather.4.cloned.1.call-update) | async-done | bytes 4194320 | tf_op jit(solution)/shard_map/all_gather | solution.py:42
  46.2 0.0 copy-done.2
  46.2 5.0 %fusion.33 = bf16[4,16,512]{2,1,0:T(8,128)(2,1)S(1)} fusion(bf16[2048,4,256]{2,1,0:T(4,128)(2,1)} %all-gather.4.cloned.1.call-done, bf16[2048,256]{0,1:T(8,128)(2,1)} %copy-done.1, bf16[2048,256]{0,1:T(8,128)(2,1)S(1)} %get-tuple-element.12, s32[4,16]{1,0:T(4,128)S(1)} %bitcast.53), kind=kOutput, calls=%fused_computation.36 | convolution fusion | flops 2169028608 | bytes 6357248 | tf_op jit(solution)/shard_map/scr,srp->scp/dot_general | solution.py:54
  51.3 0.9 copy.22
  52.2 68.9 %all-gather.6.cloned.1.call-done = bf16[16,2,256,256]{3,2,1,0:T(8,128)(2,1)} async-done(((bf16[2,2,256,256]{3,2,1,0:T(8,128)(2,1)}), bf16[16,2,256,256]{3,2,1,0:T(8,128)(2,1)}) %all-gather.6.cloned.1.call-update) | async-done | bytes 4194320 | tf_op jit(solution)/shard_map/all_gather | solution.py:61
  121.2 6.7 %fusion.18 = f32[256,2,4,256]{3,2,1,0:T(4,128)} fusion(bf16[2,4,2,16,256]{3,1,2,0,4:T(4,128)(2,1)S(1)} %copy.22, bf16[16,2,256,256,1]{3,2,1,0,4:T(8,128)(2,1)} %bitcast.51), kind=kOutput, calls=%fused_computation.30 | convolution fusion | flops 33554432 | bytes 6422528 | tf_op jit(solution)/shard_map/qspcf,cpfr->fqsr/dot_general | solution.py:58
  127.8 3.3 %all_gather_reshape.3 = f32[1,512,1024]{2,1,0:T(8,128)} reshape(f32[256,2,4,256]{3,2,1,0:T(4,128)} %fusion.18) | data formatting | bytes 4194304 | tf_op jit(solution)/shard_map/all_gather;reshape | solution.py:67
  131.2 0.0 all-gather.8.cloned.1.call-update
  131.2 8.3 %cosine_multiply_fusion = (f32[2048,256,1]{1,0,2:T(8,128)S(1)}, f32[2048,256,1]{1,0,2:T(8,128)S(1)}) fusion(s32[256]{0:T(256)S(1)} %iota_add_fusion), kind=kLoop, calls=%fused_computation.25 | loop fusion | flops 8912896 | bytes 4195328 | tf_op jit(solution)/shard_map/mul | solution.py:27
  139.5 2.9 %pad_maximum_fusion = f32[2048,256,2]{1,0,2:T(8,128)} fusion(f32[2048,256,1]{1,0,2:T(8,128)S(1)} %get-tuple-element.11, f32[2048,256,1]{1,0,2:T(8,128)S(1)} %get-tuple-element.10), kind=kLoop, calls=%fused_computation | loop fusion | flops 1048576 | bytes 8388608 | tf_op jit(solution)/shard_map/stack | solution.py:26
  142.4 7.4 %copy.18 = f32[2048,256,2]{0,2,1:T(2,128)} copy(f32[2048,256,2]{1,0,2:T(8,128)} %pad_maximum_fusion) | data formatting | bytes 8388608 | tf_op jit(solution)/shard_map/stack | solution.py:26
  149.8 6.1 %reshape.119 = f32[2048,512]{0,1:T(8,128)} reshape(f32[2048,256,2]{0,2,1:T(2,128)} %copy.18) | data formatting | bytes 8388608 | tf_op jit(solution)/shard_map/reshape | solution.py:29
  155.9 32.3 %all-gather.8.cloned.1.call-done = f32[4,512,1024]{2,1,0:T(8,128)} async-done(((f32[1,512,1024]{2,1,0:T(8,128)}), f32[4,512,1024]{2,1,0:T(8,128)}) %all-gather.8.cloned.1.call-update) | async-done | bytes 8388624 | tf_op jit(solution)/shard_map/all_gather | solution.py:67
  188.1 5.9 %reduce_sum.9 = f32[512,1024]{1,0:T(8,128)} reduce(f32[4,512,1024]{2,1,0:T(8,128)} %all-gather.8.cloned.1.call-done, f32[]{:T(128)} %constant.36.clone.1), dimensions={0}, to_apply=%region_0.1 | reduce | flops 1572864 | bytes 10485764 | tf_op jit(solution)/shard_map/reduce_sum | solution.py:68
  194.0 2.9 %copy.31 = f32[1024,512]{1,0:T(8,128)} copy(f32[1024,512]{0,1:T(8,128)} %bitcast.50) | data formatting | bytes 4194304 | tf_op jit(solution)/shard_map/dot_general | solution.py:72
  196.9 8.6 %convolution_convert_fusion = bf16[512,4,256]{2,0,1:T(8,128)(2,1)S(1)} fusion(f32[4,256,512]{2,1,0:T(8,128)} %bitcast.49, f32[2048,512]{0,1:T(8,128)} %reshape.119, s32[]{:T(128)S(6)} %select_n.30), kind=kOutput, calls=%fused_computation.31 | convolution fusion | flops 3221749760 | bytes 4194308 | tf_op jit(solution)/shard_map/dot_general | solution.py:72
  205.6 1.8 copy.25
  (4 shorter events, 0.1 us)
Async XLA Ops:
  6.5 9.9 %copy-start = (bf16[1,2,256,2048]{3,2,1,0:T(8,128)(2,1)S(1)}, bf16[1,2,256,2048]{3,2,1,0:T(8,128)(2,1)}, u32[]{:S(2)}) copy-start(bf16[1,2,256,2048]{3,2,1,0:T(8,128)(2,1)} %param.3) | copy-start | bytes 6291460
  6.5 39.6 %all-gather.4.cloned.1.call-start = ((), (), s32[]{:S(2)}) async-start(), calls=%async_computation | async-start | bytes 5242880 | tf_op jit(solution)/shard_map/all_gather | solution.py:42
  7.3 113.9 %all-gather.6.cloned.1.call-start = ((), (), s32[]{:S(2)}) async-start(), calls=%async_computation.1 | async-start | bytes 4718592 | tf_op jit(solution)/shard_map/all_gather | solution.py:61
  16.4 2.2 %copy-start.1 = (bf16[2048,256]{0,1:T(8,128)(2,1)}, bf16[2048,256]{0,1:T(8,128)(2,1)S(1)}, u32[]{:S(2)}) copy-start(bf16[2048,256]{0,1:T(8,128)(2,1)S(1)} %get-tuple-element.13) | copy-start | bytes 3145732
  16.4 29.8 %copy-start.2 = (s32[4,1,16]{2,1,0:T(1,128)S(1)}, s32[4,1,16]{2,1,0:T(1,128)}, u32[]{:S(2)}) copy-start(s32[4,1,16]{2,1,0:T(1,128)} %param.5) | copy-start | bytes 772
  18.6 169.6 %all-gather.8.cloned.1.call-start = ((), (), s32[]{:S(2)}) async-start(), calls=%async_computation.2 | async-start | bytes 10485760 | tf_op jit(solution)/shard_map/all_gather | solution.py:67
Sparse Core Ops, SparseCore 0:
  8.9 37.2 all-gather.3
  48.3 72.8 all-gather.5
  131.3 56.7 all-gather.7
